TPU v7x, 512 devices: a whole 4x4x16 slice. The times are simulated.
512 devices in a mesh: depth: 32 (over x, y, core), strip: 16 (over z).
Axes of the slice: x: 4, y: 4, z: 16, core: 2. Of those that a mesh axis runs over, the one named last changes fastest.
Arguments:
- density: float32 [128, 256, 2048], P('depth', 'strip'), may hold values from -6 to 6
- materials: int32 [128, 256, 2048], P('depth', 'strip'), may hold values from 0 to 3
- occupancy_flags: int32 [32, 16, 16], P('depth', 'strip'), may hold values from 0 to 1, as said below
- tf_color: float32 [4, 3, 16], replicated, may hold values from 0.1 to 1
- tf_opacity: float32 [4, 16], replicated, may hold values from 0.0005 to 0.05
Outputs:
- image: float32 [4, 256, 2048], P(None, 'strip', 'depth')
Inputs may be any that keep to these rules, and one draw needn't show every extreme that they name: `occupancy_flags`: occupied tiles cluster around one depth slab drawn from the seed; the share of occupied tiles differs strongly between depth slabs.
All inputs are finite; a program needn't handle non-finite values.
Results may differ from a plain program's by a relative error of at most 0.0003.
Values sent between devices are 32-bit elements; how exact they have to be, the bound alone decides.
A program may use at most 64 MiB of HBM per device.

v0:
```python
import jax
import jax.numpy as jnp
from jax import lax
from jax.sharding import PartitionSpec as P

light_x = 1.0 / 3.0
light_y = 2.0 / 3.0
light_z = 2.0 / 3.0
ambient = 0.3
diffuse = 0.7


def with_halo(array, sides, width):
    for axis, dim in sides:
        devices, length = (lax.axis_size(axis), array.shape[dim])
        up = [(i, (i + 1) % devices) for i in range(devices - 1)]
        down = [(j, i) for i, j in up]
        last = lax.slice_in_dim(array, length - width, length, axis=dim)
        first = lax.slice_in_dim(array, 0, width, axis=dim)
        before = lax.ppermute(last, axis, up)
        after = lax.ppermute(first, axis, down)
        array = jnp.concatenate([before, array, after], axis=dim)
    return array


def shade_slice(before, here, after, material_slice, occupied, knot_table):
    sample = here[1:-1, 1:-1]
    grad_z = 0.5 * (after[1:-1, 1:-1] - before[1:-1, 1:-1])
    grad_y = 0.5 * (here[2:, 1:-1] - here[:-2, 1:-1])
    grad_x = 0.5 * (here[1:-1, 2:] - here[1:-1, :-2])
    knot_count = knot_table.shape[1]
    material_count = knot_table.shape[0] // 4
    position = jnp.clip(
        (sample.reshape(-1) + 3.0) * ((knot_count - 1) / 6.0), 0.0, knot_count - 1.0
    )
    knot_grid = jnp.arange(knot_count, dtype=jnp.float32)[:, None]
    tent_weights = jnp.maximum(0.0, 1.0 - jnp.abs(position[None, :] - knot_grid))
    looked = jnp.dot(
        knot_table,
        tent_weights,
        precision=lax.Precision.HIGHEST,
        preferred_element_type=jnp.float32,
    )
    onehot = (
        material_slice.reshape(-1)[None, :] == jnp.arange(material_count, dtype=jnp.int32)[:, None]
    ).astype(jnp.float32)
    colour = jnp.sum(
        looked[: 3 * material_count].reshape(material_count, 3, -1) * onehot[:, None, :], axis=0
    )
    density_rate = jnp.sum(looked[3 * material_count :] * onehot, axis=0) * occupied.reshape(-1)
    facing = (grad_x * light_x + grad_y * light_y + grad_z * light_z).reshape(-1)
    steepness = (grad_x * grad_x + grad_y * grad_y + grad_z * grad_z).reshape(-1)
    lighting = ambient + diffuse * jnp.abs(facing) / jnp.sqrt(1.0 + steepness)
    opacity_step = 1.0 - jnp.exp(-density_rate)
    return (colour * (lighting * opacity_step)[None, :], opacity_step)


def composite_over(nearer, farther):
    return jnp.concatenate(
        [nearer[:3] + nearer[3:] * farther[:3], nearer[3:] * farther[3:]], axis=0
    )


def on_device(density, materials, occupancy_flags, tf_color, tf_opacity):
    slab_depth, row_count, columns = density.shape
    material_count = tf_color.shape[0]
    knot_count = tf_color.shape[2]
    knot_table = jnp.concatenate(
        [tf_color.reshape(material_count * 3, knot_count), tf_opacity], axis=0
    )
    padded = with_halo(density, (("depth", 0), ("strip", 1)), 1)
    padded = jnp.pad(padded, ((0, 0), (0, 0), (1, 1)))
    tile_count = occupancy_flags.shape[2]
    tile_row = jnp.repeat(occupancy_flags[0, 0], columns // tile_count).astype(jnp.float32)
    occupied = jnp.broadcast_to(tile_row[None, :], (row_count, columns))

    def advance(state_carry, slab_index):
        radiance, transmit = state_carry
        before = lax.dynamic_index_in_dim(padded, slab_index, 0, keepdims=False)
        here = lax.dynamic_index_in_dim(padded, slab_index + 1, 0, keepdims=False)
        after = lax.dynamic_index_in_dim(padded, slab_index + 2, 0, keepdims=False)
        material_slice = lax.dynamic_index_in_dim(materials, slab_index, 0, keepdims=False)
        emitted, opacity_step = shade_slice(
            before, here, after, material_slice, occupied, knot_table
        )
        return ((radiance + transmit[None, :] * emitted, transmit * (1.0 - opacity_step)), None)

    start = (
        jnp.zeros((3, row_count * columns), jnp.float32),
        jnp.ones((row_count * columns,), jnp.float32),
    )
    (radiance, transmit), _ = lax.scan(advance, start, jnp.arange(slab_depth, dtype=jnp.int32))
    partial_value = jnp.concatenate([radiance, transmit[None, :]], axis=0).reshape(
        4, row_count, columns
    )
    groups = lax.axis_size("depth")
    levels = groups.bit_length() - 1
    block_width = columns // groups
    pieces = lax.all_to_all(partial_value, "depth", split_axis=2, concat_axis=1, tiled=True)
    pieces = pieces.reshape(4, groups, row_count, block_width)
    for section_bit in range(levels):
        pieces = composite_over(pieces[:, 0::2], pieces[:, 1::2])
    finished = pieces[:, 0]
    return jnp.concatenate([finished[:3], 1.0 - finished[3:]], axis=0)


def solution(mesh):
    placed = (
        P("depth", "strip", None),
        P("depth", "strip", None),
        P("depth", "strip", None),
        P(),
        P(),
    )
    return jax.shard_map(
        on_device, mesh=mesh, in_specs=placed, out_specs=P(None, "strip", "depth"), check_vma=False
    )
```

profile of v0, /device:TPU:97, one launch (start us, length us, event | category | flops | bytes accessed | tf_op | source)
XLA Modules:
  0.0 129.5 jit_solution(18345752158085729972)
XLA Ops:
  0.0 1.0 fusion.26
  1.0 2.6 %collective-permute-start.1 = (f32[1,16,2048]{2,1,0:T(8,128)S(1)}, f32[1,16,2048]{2,1,0:T(8,128)S(1)}, u32[]{:S(2)}, u32[]{:S(2)}) collective-permute-start(f32[1,16,2048]{2,1,0:T(8,128)S(1)} %get-tuple-element.198), channel_id=1, source_target_pairs={{16,0},{32,16},{48,32},{64,48},{80,64},{96,80},{112,96},{128,112},... | collective-permute-start | bytes 393224 | tf_op jit(solution)/shard_map/ppermute | solution.py:21
  3.6 3.1 %collective-permute-start = (f32[1,16,2048]{2,1,0:T(8,128)S(1)}, f32[1,16,2048]{2,1,0:T(8,128)S(1)}, u32[]{:S(2)}, u32[]{:S(2)}) collective-permute-start(f32[1,16,2048]{2,1,0:T(8,128)S(1)} %get-tuple-element.199), channel_id=1, source_target_pairs={{0,16},{16,32},{32,48},{48,64},{64,80},{80,96},{96,112},{112,128},... | collective-permute-start | bytes 393224 | tf_op jit(solution)/shard_map/ppermute | solution.py:20
  7.4 0.7 copy.10
  8.6 1.1 constant_dynamic-update-slice_fusion.1
  9.8 4.8 %collective-permute-start.2 = (f32[6,1,2048]{2,1,0:T(1,128)S(1)}, f32[6,1,2048]{2,1,0:T(1,128)S(1)}, u32[]{:S(2)}, u32[]{:S(2)}) collective-permute-start(f32[6,1,2048]{2,1,0:T(1,128)S(1)} %get-tuple-element.194), channel_id=1, source_target_pairs={{0,1},{1,2},{2,3},{3,4},{4,5},{5,6},{6,7},{7,8},{8,9},{9,10},{10,1... | collective-permute-start | bytes 147464 | tf_op jit(solution)/shard_map/ppermute | solution.py:20
  14.6 1.9 %collective-permute-start.3 = (f32[6,1,2048]{2,1,0:T(1,128)S(1)}, f32[6,1,2048]{2,1,0:T(1,128)S(1)}, u32[]{:S(2)}, u32[]{:S(2)}) collective-permute-start(f32[6,1,2048]{2,1,0:T(1,128)S(1)} %get-tuple-element.195), channel_id=1, source_target_pairs={{1,0},{2,1},{3,2},{4,3},{5,4},{6,5},{7,6},{8,7},{9,8},{10,9},{11,1... | collective-permute-start | bytes 147464 | tf_op jit(solution)/shard_map/ppermute | solution.py:21
  16.6 4.2 %collective-permute-done.3 = f32[6,1,2048]{2,1,0:T(1,128)S(1)} collective-permute-done((f32[6,1,2048]{2,1,0:T(1,128)S(1)}, f32[6,1,2048]{2,1,0:T(1,128)S(1)}, u32[]{:S(2)}, u32[]{:S(2)}) %collective-permute-start.3) | collective-permute-done | bytes 49184 | tf_op jit(solution)/shard_map/ppermute | solution.py:21
  21.4 63.1 %while.16 = (s32[]{:T(128)}, f32[3,32768]{1,0:T(4,128)S(1)}, f32[32768]{0:T(1024)}, s32[4]{0:T(128)S(1)}, f32[6,18,2050]{2,1,0:T(8,128)S(1)}, /*index=5*/f32[16,...) while((s32[]{:T(128)}, f32[3,32768]{1,0:T(4,128)S(1)}, ...), condition=%wide.region_3.4_spmd.clone, body=%wide.region_0.3_spmd.clone.sunk | while | flops 105480208 | bytes 23315676 | solution.py:92
  27.1 0.9 dynamic-slice_bitcast_fusion.7
  28.7 2.1 %convolution_bitcast_fusion.2 = f32[16,32768]{1,0:T(8,128)S(1)} fusion(f32[16,16]{1,0:T(8,128)S(1)} %get-tuple-element.308, f32[32768]{0:T(1024)S(1)} %bitcast.78), kind=kOutput, calls=%fused_computation.1.clone.1 | convolution fusion | flops 102760448 | bytes 2229248 | tf_op jit(solution)/shard_map/while/body/eval_jaxpr/dot_general | solution.py:38
  31.3 2.1 %reshape.152 = f32[4,3,32768]{2,1,0:T(4,128)} reshape(f32[12,32768]{1,0:T(8,128)S(1)} %bitcast.70) | data formatting | bytes 3145728 | tf_op jit(solution)/shard_map/while/body/eval_jaxpr/reshape | solution.py:48
  33.4 2.4 %multiply_reduce_fusion.2 = f32[3,32768]{1,0:T(4,128)S(1)} fusion(f32[4,3,32768]{2,1,0:T(4,128)} %reshape.152, f32[4,32768]{1,0:T(4,128)S(1)} %fusion.35), kind=kLoop, calls=%fused_computation.2.clone.1 | loop fusion | flops 688128 | bytes 2490368 | tf_op jit(solution)/shard_map/while/body/eval_jaxpr/reduce_sum | solution.py:47
  42.9 0.9 dynamic-slice_bitcast_fusion.7
  44.5 2.1 %convolution_bitcast_fusion.2 = f32[16,32768]{1,0:T(8,128)S(1)} fusion(f32[16,16]{1,0:T(8,128)S(1)} %get-tuple-element.308, f32[32768]{0:T(1024)S(1)} %bitcast.78), kind=kOutput, calls=%fused_computation.1.clone.1 | convolution fusion | flops 102760448 | bytes 2229248 | tf_op jit(solution)/shard_map/while/body/eval_jaxpr/dot_general | solution.py:38
  47.1 2.1 %reshape.152 = f32[4,3,32768]{2,1,0:T(4,128)} reshape(f32[12,32768]{1,0:T(8,128)S(1)} %bitcast.70) | data formatting | bytes 3145728 | tf_op jit(solution)/shard_map/while/body/eval_jaxpr/reshape | solution.py:48
  49.1 2.4 %multiply_reduce_fusion.2 = f32[3,32768]{1,0:T(4,128)S(1)} fusion(f32[4,3,32768]{2,1,0:T(4,128)} %reshape.152, f32[4,32768]{1,0:T(4,128)S(1)} %fusion.35), kind=kLoop, calls=%fused_computation.2.clone.1 | loop fusion | flops 688128 | bytes 2490368 | tf_op jit(solution)/shard_map/while/body/eval_jaxpr/reduce_sum | solution.py:47
  58.7 0.9 dynamic-slice_bitcast_fusion.7
  60.2 2.1 %convolution_bitcast_fusion.2 = f32[16,32768]{1,0:T(8,128)S(1)} fusion(f32[16,16]{1,0:T(8,128)S(1)} %get-tuple-element.308, f32[32768]{0:T(1024)S(1)} %bitcast.78), kind=kOutput, calls=%fused_computation.1.clone.1 | convolution fusion | flops 102760448 | bytes 2229248 | tf_op jit(solution)/shard_map/while/body/eval_jaxpr/dot_general | solution.py:38
  62.8 2.1 %reshape.152 = f32[4,3,32768]{2,1,0:T(4,128)} reshape(f32[12,32768]{1,0:T(8,128)S(1)} %bitcast.70) | data formatting | bytes 3145728 | tf_op jit(solution)/shard_map/while/body/eval_jaxpr/reshape | solution.py:48
  64.9 2.4 %multiply_reduce_fusion.2 = f32[3,32768]{1,0:T(4,128)S(1)} fusion(f32[4,3,32768]{2,1,0:T(4,128)} %reshape.152, f32[4,32768]{1,0:T(4,128)S(1)} %fusion.35), kind=kLoop, calls=%fused_computation.2.clone.1 | loop fusion | flops 688128 | bytes 2490368 | tf_op jit(solution)/shard_map/while/body/eval_jaxpr/reduce_sum | solution.py:47
  74.4 0.9 dynamic-slice_bitcast_fusion.7
  76.0 2.1 %convolution_bitcast_fusion.2 = f32[16,32768]{1,0:T(8,128)S(1)} fusion(f32[16,16]{1,0:T(8,128)S(1)} %get-tuple-element.308, f32[32768]{0:T(1024)S(1)} %bitcast.78), kind=kOutput, calls=%fused_computation.1.clone.1 | convolution fusion | flops 102760448 | bytes 2229248 | tf_op jit(solution)/shard_map/while/body/eval_jaxpr/dot_general | solution.py:38
  78.6 2.1 %reshape.152 = f32[4,3,32768]{2,1,0:T(4,128)} reshape(f32[12,32768]{1,0:T(8,128)S(1)} %bitcast.70) | data formatting | bytes 3145728 | tf_op jit(solution)/shard_map/while/body/eval_jaxpr/reshape | solution.py:48
  80.6 2.4 %multiply_reduce_fusion.2 = f32[3,32768]{1,0:T(4,128)S(1)} fusion(f32[4,3,32768]{2,1,0:T(4,128)} %reshape.152, f32[4,32768]{1,0:T(4,128)S(1)} %fusion.35), kind=kLoop, calls=%fused_computation.2.clone.1 | loop fusion | flops 688128 | bytes 2490368 | tf_op jit(solution)/shard_map/while/body/eval_jaxpr/reduce_sum | solution.py:47
  84.4 0.9 concatenate.35
  85.7 3.1 %copy.11 = f32[4,16,2048]{1,0,2:T(4,128)} copy(f32[4,16,2048]{2,1,0:T(8,128)S(1)} %pad_maximum_fusion) | data formatting | bytes 1048576 | tf_op jit(solution)/shard_map/concatenate | solution.py:93
  88.7 4.8 %reshape.149 = f32[32,1,4096]{2,1,0:T(1,128)S(1)} reshape(f32[2048,4,16]{2,1,0:T(4,128)} %bitcast.75) | data formatting | bytes 1048576
  93.5 23.0 %all_to_all.15 = f32[32,1,4096]{2,1,0:T(1,128)S(1)} all-to-all(f32[32,1,4096]{2,1,0:T(1,128)S(1)} %reshape.149), channel_id=1, replica_groups=mesh['depth'=32,'strip'=16] {'depth'}, dimensions={0} | all-to-all | bytes 1048576 | tf_op jit(solution)/shard_map/all_to_all | solution.py:99
  117.0 1.9 %reduce = f32[32,4096]{1,0:T(8,128)S(1)} reduce(f32[32,1,4096]{2,1,0:T(1,128)S(1)} %all_to_all.15, f32[]{:T(128)} %broadcast.229), dimensions={1}, to_apply=%all_to_all.11.reduce_sub_computation | reduce | bytes 1048580 | tf_op jit(solution)/shard_map/all_to_all | solution.py:99
  118.9 4.3 %reshape.150 = f32[2048,4,16]{2,1,0:T(4,128)} reshape(f32[32,4096]{1,0:T(8,128)S(1)} %reduce) | data formatting | bytes 1048576
  123.2 3.5 %copy.13 = f32[4,16,32,64]{3,2,1,0:T(8,128)S(1)} copy(f32[4,16,32,64]{1,0,3,2:T(4,128)} %bitcast.74) | data formatting | bytes 1048576 | tf_op jit(solution)/shard_map/all_to_all | solution.py:99
  (137 shorter events, 17.4 us)
Async XLA Ops:
  0.0 16.5 %copy-start.4 = (f32[4,16]{1,0:T(4,128)S(1)}, f32[4,16]{1,0:T(4,128)}, u32[]{:S(2)}) copy-start(f32[4,16]{1,0:T(4,128)} %param.11) | copy-start | bytes 772
  1.0 8.7 %collective-permute-start.1 = (f32[1,16,2048]{2,1,0:T(8,128)S(1)}, f32[1,16,2048]{2,1,0:T(8,128)S(1)}, u32[]{:S(2)}, u32[]{:S(2)}) collective-permute-start(f32[1,16,2048]{2,1,0:T(8,128)S(1)} %get-tuple-element.198), channel_id=1, source_target_pairs={{16,0},{32,16},{48,32},{64,48},{80,64},{96,80},{112,96},{128,112},... | collective-permute-start | bytes 393224 | tf_op jit(solution)/shard_map/ppermute | solution.py:21
  3.6 5.0 %collective-permute-start = (f32[1,16,2048]{2,1,0:T(8,128)S(1)}, f32[1,16,2048]{2,1,0:T(8,128)S(1)}, u32[]{:S(2)}, u32[]{:S(2)}) collective-permute-start(f32[1,16,2048]{2,1,0:T(8,128)S(1)} %get-tuple-element.199), channel_id=1, source_target_pairs={{0,16},{16,32},{32,48},{48,64},{64,80},{80,96},{96,112},{112,128},... | collective-permute-start | bytes 393224 | tf_op jit(solution)/shard_map/ppermute | solution.py:20
  9.8 6.7 %collective-permute-start.2 = (f32[6,1,2048]{2,1,0:T(1,128)S(1)}, f32[6,1,2048]{2,1,0:T(1,128)S(1)}, u32[]{:S(2)}, u32[]{:S(2)}) collective-permute-start(f32[6,1,2048]{2,1,0:T(1,128)S(1)} %get-tuple-element.194), channel_id=1, source_target_pairs={{0,1},{1,2},{2,3},{3,4},{4,5},{5,6},{6,7},{7,8},{8,9},{9,10},{10,1... | collective-permute-start | bytes 147464 | tf_op jit(solution)/shard_map/ppermute | solution.py:20
  14.6 6.1 %collective-permute-start.3 = (f32[6,1,2048]{2,1,0:T(1,128)S(1)}, f32[6,1,2048]{2,1,0:T(1,128)S(1)}, u32[]{:S(2)}, u32[]{:S(2)}) collective-permute-start(f32[6,1,2048]{2,1,0:T(1,128)S(1)} %get-tuple-element.195), channel_id=1, source_target_pairs={{1,0},{2,1},{3,2},{4,3},{5,4},{6,5},{7,6},{8,7},{9,8},{10,9},{11,1... | collective-permute-start | bytes 147464 | tf_op jit(solution)/shard_map/ppermute | solution.py:21
  21.4 6.8 %copy-start.5 = (s32[4]{0:T(128)}, s32[4]{0:T(128)S(1)}, u32[]{:S(2)}) copy-start(s32[4]{0:T(128)S(1)} %get-tuple-element.306) | copy-start | bytes 52 | tf_op jit(solution)/shard_map/while
  21.4 7.3 %copy-start = (f32[6,18,2050]{2,1,0:T(8,128)}, f32[6,18,2050]{2,1,0:T(8,128)S(1)}, u32[]{:S(2)}) copy-start(f32[6,18,2050]{2,1,0:T(8,128)S(1)} %get-tuple-element.307) | copy-start | bytes 2656804 | tf_op jit(solution)/shard_map/while
  33.4 2.5 %copy-start.2 = (f32[32768]{0:T(1024)S(1)}, f32[32768]{0:T(1024)}, u32[]{:S(2)}) copy-start(f32[32768]{0:T(1024)} %get-tuple-element.290) | copy-start | bytes 393220 | tf_op jit(solution)/shard_map/while
  35.8 1.3 %copy-start.1 = (f32[6,18,2050]{2,1,0:T(8,128)S(1)}, f32[6,18,2050]{2,1,0:T(8,128)}, u32[]{:S(2)}) copy-start(f32[6,18,2050]{2,1,0:T(8,128)} %copy-done) | copy-start | bytes 2656804 | tf_op jit(solution)/shard_map/while
  35.8 1.3 %copy-start.6 = (s32[4]{0:T(128)S(1)}, s32[4]{0:T(128)}, u32[]{:S(2)}) copy-start(s32[4]{0:T(128)} %copy-done.5) | copy-start | bytes 52 | tf_op jit(solution)/shard_map/while
  35.9 0.7 copy-start.3
  37.2 6.7 %copy-start.5 = (s32[4]{0:T(128)}, s32[4]{0:T(128)S(1)}, u32[]{:S(2)}) copy-start(s32[4]{0:T(128)S(1)} %get-tuple-element.306) | copy-start | bytes 52 | tf_op jit(solution)/shard_map/while
  37.2 7.3 %copy-start = (f32[6,18,2050]{2,1,0:T(8,128)}, f32[6,18,2050]{2,1,0:T(8,128)S(1)}, u32[]{:S(2)}) copy-start(f32[6,18,2050]{2,1,0:T(8,128)S(1)} %get-tuple-element.307) | copy-start | bytes 2656804 | tf_op jit(solution)/shard_map/while
  49.1 2.5 %copy-start.2 = (f32[32768]{0:T(1024)S(1)}, f32[32768]{0:T(1024)}, u32[]{:S(2)}) copy-start(f32[32768]{0:T(1024)} %get-tuple-element.290) | copy-start | bytes 393220 | tf_op jit(solution)/shard_map/while
  51.6 1.3 %copy-start.1 = (f32[6,18,2050]{2,1,0:T(8,128)S(1)}, f32[6,18,2050]{2,1,0:T(8,128)}, u32[]{:S(2)}) copy-start(f32[6,18,2050]{2,1,0:T(8,128)} %copy-done) | copy-start | bytes 2656804 | tf_op jit(solution)/shard_map/while
  51.6 1.3 %copy-start.6 = (s32[4]{0:T(128)S(1)}, s32[4]{0:T(128)}, u32[]{:S(2)}) copy-start(s32[4]{0:T(128)} %copy-done.5) | copy-start | bytes 52 | tf_op jit(solution)/shard_map/while
  51.7 0.7 copy-start.3
  52.9 6.7 %copy-start.5 = (s32[4]{0:T(128)}, s32[4]{0:T(128)S(1)}, u32[]{:S(2)}) copy-start(s32[4]{0:T(128)S(1)} %get-tuple-element.306) | copy-start | bytes 52 | tf_op jit(solution)/shard_map/while
  52.9 7.3 %copy-start = (f32[6,18,2050]{2,1,0:T(8,128)}, f32[6,18,2050]{2,1,0:T(8,128)S(1)}, u32[]{:S(2)}) copy-start(f32[6,18,2050]{2,1,0:T(8,128)S(1)} %get-tuple-element.307) | copy-start | bytes 2656804 | tf_op jit(solution)/shard_map/while
  64.9 2.5 %copy-start.2 = (f32[32768]{0:T(1024)S(1)}, f32[32768]{0:T(1024)}, u32[]{:S(2)}) copy-start(f32[32768]{0:T(1024)} %get-tuple-element.290) | copy-start | bytes 393220 | tf_op jit(solution)/shard_map/while
  67.3 1.3 %copy-start.1 = (f32[6,18,2050]{2,1,0:T(8,128)S(1)}, f32[6,18,2050]{2,1,0:T(8,128)}, u32[]{:S(2)}) copy-start(f32[6,18,2050]{2,1,0:T(8,128)} %copy-done) | copy-start | bytes 2656804 | tf_op jit(solution)/shard_map/while
  67.3 1.3 %copy-start.6 = (s32[4]{0:T(128)S(1)}, s32[4]{0:T(128)}, u32[]{:S(2)}) copy-start(s32[4]{0:T(128)} %copy-done.5) | copy-start | bytes 52 | tf_op jit(solution)/shard_map/while
  67.4 0.7 copy-start.3
  68.7 6.7 %copy-start.5 = (s32[4]{0:T(128)}, s32[4]{0:T(128)S(1)}, u32[]{:S(2)}) copy-start(s32[4]{0:T(128)S(1)} %get-tuple-element.306) | copy-start | bytes 52 | tf_op jit(solution)/shard_map/while
  68.7 7.3 %copy-start = (f32[6,18,2050]{2,1,0:T(8,128)}, f32[6,18,2050]{2,1,0:T(8,128)S(1)}, u32[]{:S(2)}) copy-start(f32[6,18,2050]{2,1,0:T(8,128)S(1)} %get-tuple-element.307) | copy-start | bytes 2656804 | tf_op jit(solution)/shard_map/while
  80.6 2.5 %copy-start.2 = (f32[32768]{0:T(1024)S(1)}, f32[32768]{0:T(1024)}, u32[]{:S(2)}) copy-start(f32[32768]{0:T(1024)} %get-tuple-element.290) | copy-start | bytes 393220 | tf_op jit(solution)/shard_map/while
  83.1 1.3 %copy-start.1 = (f32[6,18,2050]{2,1,0:T(8,128)S(1)}, f32[6,18,2050]{2,1,0:T(8,128)}, u32[]{:S(2)}) copy-start(f32[6,18,2050]{2,1,0:T(8,128)} %copy-done) | copy-start | bytes 2656804 | tf_op jit(solution)/shard_map/while
  83.1 1.3 %copy-start.6 = (s32[4]{0:T(128)S(1)}, s32[4]{0:T(128)}, u32[]{:S(2)}) copy-start(s32[4]{0:T(128)} %copy-done.5) | copy-start | bytes 52 | tf_op jit(solution)/shard_map/while
  83.2 0.7 copy-start.3
where the time goes:
time: 131 us; the launch traced here: 130 us
  local copies, waits for them, and re-layouts  40.5 us (31%)
  blocking collectives  23 us (18%)
  loops' own time  20.8 us (16%)
  other arithmetic  19.3 us (15%)
  starting transfers between devices  12.4 us (9%)
  matrix products  8.57 us (7%)
  waiting for transfers between devices  4.66 us (4%)
    all_to_all x1, blocking collectives, on_device(): lax.all_to_all(partial_value, 'depth', split_axis=2, concat_axis=1, tiled...  23 us
    another operation x1, loops' own time, on_device(): lax.scan(advance, start, jnp.arange(slab_depth, dtype=jnp.int32))  20.8 us
    unnamed x8, local copies, waits for them, and re-layouts  11.1 us
    reduce_sum x4, other arithmetic, shade_slice(): jnp.sum(looked[:3 * material_count].reshape(material_count, 3, -1) * oneh...  9.79 us
    dot_general x4, matrix products, shade_slice(): jnp.dot(knot_table, tent_weights, precision=lax.Precision.HIGHEST, prefer...  8.57 us
    reshape x4, local copies, waits for them, and re-layouts, shade_slice(): looked[:3 * material_count].reshape(material_count, 3, -1)  8.23 us
    ppermute x2, starting transfers between devices, with_halo(): before = lax.ppermute(last, axis, up)  7.86 us
    while x72, local copies, waits for them, and re-layouts  7.4 us
  transfers between devices with their start and end apart: 4, of which 2 were waited for; matrix products, arithmetic and copies ran while one was open for 2% of the time, Pallas kernels for 0%

commit v1 on v0

v1 whole, which is shorter than its diff:
```python
import jax
import jax.numpy as jnp
from jax import lax
from jax.experimental import pallas as pl
from jax.experimental.pallas import tpu as pltpu
from jax.sharding import PartitionSpec as P

MESH = pl.DeviceIdType.MESH
LANES = 128
HALF = LANES // 2
SIDE = 4
CHIPS = SIDE * SIDE
ORDER = (2, 1, 3, 0)


def kernel(
    density, materials, flags, tf_color, tf_opacity, image,
    field, mats, top, bottom, shade, through, packed, outgoing, pieces,
    load_sem, plane_send, plane_recv, row_send, row_recv,
    core_send, core_recv, piece_send, piece_recv,
):
    depth_count = lax.axis_size("depth")
    strip_count = lax.axis_size("strip")
    d = lax.axis_index("depth")
    s = lax.axis_index("strip")
    core = lax.rem(d, 2)
    chip = d // 2
    chip_x = chip // SIDE
    partner = d + 1 - 2 * core
    cross = d - 1 + 2 * core
    cross_ok = jnp.logical_and(cross >= 0, cross < depth_count)
    planes, rows, columns = density.shape
    chunk = columns // SIDE
    tiles = columns // LANES
    per_chunk = chunk // LANES

    barrier = pltpu.get_barrier_semaphore()

    def greet(**where):
        pl.semaphore_signal(barrier, inc=1, device_id=where, device_id_type=MESH)

    greet(depth=partner)
    pl.when(cross_ok)(lambda: greet(depth=cross))
    pl.when(s > 0)(lambda: greet(strip=s - 1))
    pl.when(s < strip_count - 1)(lambda: greet(strip=s + 1))

    @pl.loop(0, CHIPS)
    def _(k):
        pl.when(k != chip)(lambda: greet(depth=2 * k + core))

    def load(j):
        cols = pl.ds(j * chunk, chunk)
        return (
            pltpu.make_async_copy(
                density.at[:, :, cols],
                field.at[pl.ds(1, planes), :, pl.ds(j * chunk + LANES, chunk)],
                load_sem.at[0, j],
            ),
            pltpu.make_async_copy(
                materials.at[:, :, cols], mats.at[:, :, cols], load_sem.at[1, j]
            ),
        )

    for j in range(SIDE):
        for copy in load(j):
            copy.start()

    edge = jnp.zeros((planes, rows, LANES), jnp.float32)
    field[pl.ds(1, planes), :, pl.ds(0, LANES)] = edge
    field[pl.ds(1, planes), :, pl.ds(columns + LANES, LANES)] = edge

    expected = (
        CHIPS
        + cross_ok.astype(jnp.int32)
        + (s > 0).astype(jnp.int32)
        + (s < strip_count - 1).astype(jnp.int32)
    )
    pl.semaphore_wait(barrier, expected)

    def plane_copy(way, j):
        j = pl.multiple_of(j * chunk, LANES)
        source = planes - 1 if way == 0 else 0
        target = 0 if way == 0 else planes + 1
        at = j // chunk
        return pltpu.make_async_remote_copy(
            src_ref=density.at[source, :, pl.ds(j, chunk)],
            dst_ref=field.at[target, :, pl.ds(j + LANES, chunk)],
            send_sem=plane_send.at[way, at],
            recv_sem=plane_recv.at[way, at],
            device_id={"depth": d + 1 if way == 0 else d - 1},
            device_id_type=MESH,
        )

    def row_copy(way):
        source = rows - 1 if way == 0 else 0
        return pltpu.make_async_remote_copy(
            src_ref=density.at[:, pl.ds(source, 1), :],
            dst_ref=top if way == 0 else bottom,
            send_sem=row_send.at[way],
            recv_sem=row_recv.at[way],
            device_id={"strip": s + 1 if way == 0 else s - 1},
            device_id_type=MESH,
        )

    has_next = d < depth_count - 1
    has_before = d > 0
    has_below = s < strip_count - 1
    has_above = s > 0

    def owner(j):
        return lax.rem(chip_x + ORDER[j], SIDE)

    pl.when(has_below)(lambda: row_copy(0).start())
    pl.when(has_above)(lambda: row_copy(1).start())
    for j in range(SIDE):
        pl.when(has_next)(lambda: plane_copy(0, owner(j)).start())
        pl.when(has_before)(lambda: plane_copy(1, owner(j)).start())

    @pl.when(jnp.logical_not(has_before))
    def _():
        field[0] = jnp.zeros(field.shape[1:], jnp.float32)

    @pl.when(jnp.logical_not(has_next))
    def _():
        field[planes + 1] = jnp.zeros(field.shape[1:], jnp.float32)

    @pl.when(jnp.logical_not(has_above))
    def _():
        top[...] = jnp.zeros(top.shape, jnp.float32)

    @pl.when(jnp.logical_not(has_below))
    def _():
        bottom[...] = jnp.zeros(bottom.shape, jnp.float32)

    material_count, _, knots = tf_color.shape
    lane = lax.broadcasted_iota(jnp.int32, (8, LANES), 1)
    sub = lax.broadcasted_iota(jnp.int32, (8, LANES), 0)

    def table(row_of):
        parts = [row_of(m) for m in range(material_count)]
        parts.append(jnp.zeros((1, LANES - material_count * knots), jnp.float32))
        base = jnp.broadcast_to(jnp.concatenate(parts, axis=1), (8, LANES))
        return base, pltpu.roll(base, LANES - 1, 1) - base

    tables = [table(lambda m, c=c: tf_color[m, pl.ds(c, 1), :]) for c in range(3)]
    tables.append(table(lambda m: tf_opacity[pl.ds(m, 1), :]))

    def look(entry, index):
        return jnp.take_along_axis(entry, index, axis=1, mode="promise_in_bounds")

    for j in range(SIDE):
        for copy in load(j):
            copy.wait()

        @pl.loop(j * per_chunk, (j + 1) * per_chunk)
        def _(t):
            at = pl.multiple_of(t * LANES, LANES)
            occupied = flags[0, 0, t].astype(jnp.float32)
            for half in range(rows // 8):
                band = pl.ds(8 * half, 8)
                passed = jnp.ones((8, LANES), jnp.float32)
                for z in range(planes):
                    sample = field[z + 1, band, pl.ds(at + LANES, LANES)]
                    position = jnp.clip((sample + 3.0) * ((knots - 1) / 6.0), 0.0, knots - 1.0)
                    knot = position.astype(jnp.int32)
                    part = position - knot.astype(jnp.float32)
                    index = (mats[z, band, pl.ds(at, LANES)] * knots + knot) & (LANES - 1)
                    values = [look(b, index) + part * look(g, index) for b, g in tables]
                    kept = jnp.exp(-(values[3] * occupied))
                    weight = passed * (1.0 - kept)
                    for c in range(3):
                        shade[c, z, band, pl.ds(at, LANES)] = values[c] * weight
                    passed = passed * kept
                through[band, pl.ds(at, LANES)] = passed

    pl.when(has_above)(lambda: row_copy(0).wait_recv())
    pl.when(has_below)(lambda: row_copy(1).wait_recv())

    def core_copy(j):
        mine = pl.ds(j * per_chunk, per_chunk)
        return pltpu.make_async_remote_copy(
            src_ref=packed.at[1 - core, mine],
            dst_ref=packed.at[2, mine],
            send_sem=core_send.at[j],
            recv_sem=core_recv.at[j],
            device_id={"depth": partner},
            device_id_type=MESH,
        )

    def piece_copy(k, source):
        return pltpu.make_async_remote_copy(
            src_ref=outgoing.at[k],
            dst_ref=pieces.at[source],
            send_sem=piece_send.at[k],
            recv_sem=piece_recv.at[source],
            device_id={"depth": 2 * k + core},
            device_id_type=MESH,
        )

    def light_tile(t):
        at = pl.multiple_of(t * LANES, LANES)

        def tile(z, half, shift=0):
            return field[z, pl.ds(8 * half, 8), pl.ds(at + LANES + shift * LANES, LANES)]

        sums = [[None] * 4 for _ in range(2)]
        for half in range(2):
            sums[half][3] = through[pl.ds(8 * half, 8), pl.ds(at, LANES)]
        column = [[tile(z, half) for half in range(2)] for z in range(planes + 2)]
        for z in range(planes):
            above = jnp.broadcast_to(top[z, :, pl.ds(at, LANES)], (8, LANES))
            below = jnp.broadcast_to(bottom[z, :, pl.ds(at, LANES)], (8, LANES))
            here = column[z + 1]
            for half in range(2):
                mid = here[half]
                left = pltpu.roll(jnp.where(lane == LANES - 1, tile(z + 1, half, -1), mid), 1, 1)
                right = pltpu.roll(jnp.where(lane == 0, tile(z + 1, half, 1), mid), LANES - 1, 1)
                up = pltpu.roll(jnp.where(sub == 7, above if half == 0 else here[0], mid), 1, 0)
                down = pltpu.roll(jnp.where(sub == 0, below if half == 1 else here[1], mid), 7, 0)
                gx = right - left
                gy = down - up
                gz = column[z + 2][half] - column[z][half]
                facing = gx + 2.0 * (gy + gz)
                steep = gx * gx + gy * gy + gz * gz
                light = 0.3 + (0.7 / 3.0) * jnp.abs(facing) * lax.rsqrt(4.0 + steep)
                for c in range(3):
                    term = shade[c, z, pl.ds(8 * half, 8), pl.ds(at, LANES)] * light
                    sums[half][c] = term if z == 0 else sums[half][c] + term
        return sums

    def pack(j):
        @pl.loop(0, per_chunk)
        def _(y):
            sums = light_tile(owner(j) * per_chunk + y)
            for c in range(4):
                first, second = sums[0][c], sums[1][c]
                packed[0, j * per_chunk + y, c] = jnp.where(
                    lane < HALF, first, pltpu.roll(second, HALF, 1)
                )
                packed[1, j * per_chunk + y, c] = jnp.where(
                    lane < HALF, pltpu.roll(first, HALF, 1), second
                )

    def join(j):
        core_copy(j).wait_recv()

        @pl.loop(0, per_chunk)
        def _(y):
            k = owner(j) * SIDE + y
            near = packed.at[2 * core, j * per_chunk + y]
            far = packed.at[2 - core, j * per_chunk + y]
            passed = near[3]
            for c in range(3):
                outgoing[k, c] = near[c] + passed * far[c]
            outgoing[k, 3] = passed * far[3]

        @pl.loop(0, per_chunk)
        def _(y):
            k = owner(j) * SIDE + y
            pl.when(k != chip)(lambda: piece_copy(k, chip).start())

    for j in range(SIDE):
        pl.when(has_before)(lambda: plane_copy(0, owner(j)).wait_recv())
        pl.when(has_next)(lambda: plane_copy(1, owner(j)).wait_recv())
        pack(j)
        core_copy(j).start()
        if j > 0:
            join(j - 1)
    join(SIDE - 1)

    pieces[chip] = outgoing[chip]

    @pl.loop(0, CHIPS)
    def _(k):
        pl.when(k != chip)(lambda: piece_copy(k, k).wait_recv())

    def over(k, held):
        passed = held[3]
        return tuple(held[c] + passed * pieces[k, c] for c in range(3)) + (
            passed * pieces[k, 3],
        )

    start = tuple(pieces[0, c] for c in range(4))
    held = lax.fori_loop(1, CHIPS, over, start)
    for c in range(4):
        value = held[c] if c < 3 else 1.0 - held[c]
        image[c, pl.ds(0, 8), :] = value[:, :HALF]
        image[c, pl.ds(8, 8), :] = pltpu.roll(value, HALF, 1)[:, :HALF]

    pl.when(has_below)(lambda: row_copy(0).wait_send())
    pl.when(has_above)(lambda: row_copy(1).wait_send())
    for j in range(SIDE):
        pl.when(has_next)(lambda: plane_copy(0, owner(j)).wait_send())
        pl.when(has_before)(lambda: plane_copy(1, owner(j)).wait_send())
        core_copy(j).wait_send()

    @pl.loop(0, CHIPS)
    def _(k):
        pl.when(k != chip)(lambda: piece_copy(k, chip).wait_send())


def on_device(density, materials, occupancy_flags, tf_color, tf_opacity):
    planes, rows, columns = density.shape
    tiles = columns // LANES
    block = (4, 8, LANES)
    f32 = jnp.float32
    dma = pltpu.SemaphoreType.DMA
    return pl.pallas_call(
        kernel,
        out_shape=jax.ShapeDtypeStruct((4, rows, columns // lax.axis_size("depth")), f32),
        in_specs=[
            pl.BlockSpec(memory_space=pltpu.HBM),
            pl.BlockSpec(memory_space=pltpu.HBM),
            pl.BlockSpec(memory_space=pltpu.SMEM),
            pl.BlockSpec(memory_space=pltpu.VMEM),
            pl.BlockSpec(memory_space=pltpu.VMEM),
        ],
        out_specs=pl.BlockSpec(memory_space=pltpu.VMEM),
        scratch_shapes=[
            pltpu.VMEM((planes + 2, rows, columns + 2 * LANES), f32),
            pltpu.VMEM((planes, rows, columns), jnp.int32),
            pltpu.VMEM((planes, 1, columns), f32),
            pltpu.VMEM((planes, 1, columns), f32),
            pltpu.VMEM((3, planes, rows, columns), f32),
            pltpu.VMEM((rows, columns), f32),
            pltpu.VMEM((3, tiles) + block, f32),
            pltpu.VMEM((CHIPS,) + block, f32),
            pltpu.VMEM((CHIPS,) + block, f32),
            dma((2, SIDE)),
            dma((2, SIDE)),
            dma((2, SIDE)),
            dma((2,)),
            dma((2,)),
            dma((SIDE,)),
            dma((SIDE,)),
            dma((CHIPS,)),
            dma((CHIPS,)),
        ],
        compiler_params=pltpu.CompilerParams(
            collective_id=0, has_side_effects=True, vmem_limit_bytes=60 << 20
        ),
        name="render",
    )(density, materials, occupancy_flags, tf_color, tf_opacity)


def solution(mesh):
    placed = (
        P("depth", "strip", None),
        P("depth", "strip", None),
        P("depth", "strip", None),
        P(),
        P(),
    )
    return jax.shard_map(
        on_device, mesh=mesh, in_specs=placed, out_specs=P(None, "strip", "depth"), check_vma=False
    )
```

time: 131 us -> 27.1 us (0.21)
  the two profiles are of different devices: /device:TPU:97 before, /device:TPU:1 now
where the time goes in v1:
time: 27.1 us; the launch traced here: 26.8 us
  Pallas kernels  24.1 us (89%)
  local copies, waits for them, and re-layouts  2.67 us (10%)
    pallas_call x1, Pallas kernels, on_device(): pl.pallas_call(kernel, out_shape=jax.ShapeDtypeStruct((4, rows, columns /...  24.1 us
    unnamed x2, local copies, waits for them, and re-layouts  2.67 us

profile of v1, /device:TPU:1, one launch (start us, length us, event | category | flops | bytes accessed | tf_op | source)
XLA Modules:
  0.0 26.8 jit_solution(15756796010617255080)
XLA Ops:
  0.0 1.3 %copy.6.tf_color = f32[4,3,16]{2,1,0:T(4,128)} copy(f32[4,3,16]{2,0,1:T(4,128)} %param.8) | data formatting | bytes 1536 | tf_op args[3]
  1.3 24.1 %render.1 = f32[4,16,64]{2,1,0:T(8,128)} custom-call(f32[4,16,2048]{2,1,0:T(8,128)} %density.1, s32[4,16,2048]{2,1,0:T(8,128)} %materials.1, s32[1,1,16]{2,1,0:T(1,128)} %flags.1, f32[4,3,16]{2,1,0:T(4,128)} %copy.6.tf_color, f32[4,16]{1,0:T(4,128)} %tf_opacity.1), custom_call_target="tpu_custom_call" | custom-call | tf_op jit(solution)/shard_map/render/pallas_call | solution.py:308
  25.4 1.4 %copy.8 = f32[4,16,64]{2,1,0:T(8,128)} copy(f32[4,16,64]{2,1,0:T(8,128)} %render.1) | data formatting | bytes 32768

commit v2 on v1

--- a/solution.py
+++ b/solution.py
@@ -10,12 +10,15 @@
 HALF = LANES // 2
 SIDE = 4
 CHIPS = SIDE * SIDE
+LOOK_UNROLL = 4
+LIGHT_UNROLL = 2
 ORDER = (2, 1, 3, 0)
 
 
 def kernel(
-    density, materials, flags, tf_color, tf_opacity, image,
+    density, materials, flags_in, color_in, opacity_in, image,
     field, mats, top, bottom, shade, through, packed, outgoing, pieces,
+    looked, flags, tf_color, tf_opacity, small_sem, relay,
     load_sem, plane_send, plane_recv, row_send, row_recv,
     core_send, core_recv, piece_send, piece_recv,
 ):
@@ -34,26 +37,32 @@
     tiles = columns // LANES
     per_chunk = chunk // LANES
 
+    chip_y = lax.rem(chip, SIDE)
+
+    def on_chip(x, y):
+        return 2 * (lax.rem(x, SIDE) * SIDE + lax.rem(y, SIDE)) + core
+
+    along_x = [on_chip(chip_x + step, chip_y) for step in (1, SIDE - 1)]
+    along_y = [on_chip(chip_x, chip_y + step) for step in (1, SIDE - 1)]
     barrier = pltpu.get_barrier_semaphore()
 
-    def greet(**where):
-        pl.semaphore_signal(barrier, inc=1, device_id=where, device_id_type=MESH)
-
-    greet(depth=partner)
-    pl.when(cross_ok)(lambda: greet(depth=cross))
-    pl.when(s > 0)(lambda: greet(strip=s - 1))
-    pl.when(s < strip_count - 1)(lambda: greet(strip=s + 1))
-
-    @pl.loop(0, CHIPS)
-    def _(k):
-        pl.when(k != chip)(lambda: greet(depth=2 * k + core))
+    def tell(sem, **where):
+        pl.semaphore_signal(sem, inc=1, device_id=where, device_id_type=MESH)
+
+    pl.when(cross_ok)(lambda: tell(barrier, depth=cross))
+    pl.when(s > 0)(lambda: tell(barrier, strip=s - 1))
+    pl.when(s < strip_count - 1)(lambda: tell(barrier, strip=s + 1))
+    tell(barrier, depth=partner)
+    for other in along_x + along_y:
+        tell(barrier, depth=other)
 
     def load(j):
-        cols = pl.ds(j * chunk, chunk)
+        start = pl.multiple_of(j * chunk, LANES)
+        cols = pl.ds(start, chunk)
         return (
             pltpu.make_async_copy(
                 density.at[:, :, cols],
-                field.at[pl.ds(1, planes), :, pl.ds(j * chunk + LANES, chunk)],
+                field.at[pl.ds(1, planes), :, pl.ds(start + LANES, chunk)],
                 load_sem.at[0, j],
             ),
             pltpu.make_async_copy(
@@ -61,6 +70,13 @@
             ),
         )
 
+    small = (
+        pltpu.make_async_copy(flags_in, flags, small_sem.at[0]),
+        pltpu.make_async_copy(color_in, tf_color, small_sem.at[1]),
+        pltpu.make_async_copy(opacity_in, tf_opacity, small_sem.at[2]),
+    )
+    for copy in small:
+        copy.start()
     for j in range(SIDE):
         for copy in load(j):
             copy.start()
@@ -70,7 +86,9 @@
     field[pl.ds(1, planes), :, pl.ds(columns + LANES, LANES)] = edge
 
     expected = (
-        CHIPS
+        1
+        + len(along_x)
+        + len(along_y)
         + cross_ok.astype(jnp.int32)
         + (s > 0).astype(jnp.int32)
         + (s < strip_count - 1).astype(jnp.int32)
@@ -116,6 +134,15 @@
         pl.when(has_next)(lambda: plane_copy(0, owner(j)).start())
         pl.when(has_before)(lambda: plane_copy(1, owner(j)).start())
 
+    def relay_on(step, others):
+        for other in others:
+            tell(relay.at[step], depth=other)
+
+    def relayed(step):
+        pl.semaphore_wait(relay.at[step], 2)
+
+    relay_on(0, along_y)
+
     @pl.when(jnp.logical_not(has_before))
     def _():
         field[0] = jnp.zeros(field.shape[1:], jnp.float32)
@@ -132,7 +159,9 @@
     def _():
         bottom[...] = jnp.zeros(bottom.shape, jnp.float32)
 
-    material_count, _, knots = tf_color.shape
+    _, material_count, knots = tf_color.shape
+    for copy in small:
+        copy.wait()
     lane = lax.broadcasted_iota(jnp.int32, (8, LANES), 1)
     sub = lax.broadcasted_iota(jnp.int32, (8, LANES), 0)
 
@@ -142,36 +171,86 @@
         base = jnp.broadcast_to(jnp.concatenate(parts, axis=1), (8, LANES))
         return base, pltpu.roll(base, LANES - 1, 1) - base
 
-    tables = [table(lambda m, c=c: tf_color[m, pl.ds(c, 1), :]) for c in range(3)]
+    tables = [table(lambda m, c=c: tf_color[c, pl.ds(m, 1), :]) for c in range(3)]
     tables.append(table(lambda m: tf_opacity[pl.ds(m, 1), :]))
 
+    along_lanes = lax.GatherDimensionNumbers(
+        offset_dims=(),
+        collapsed_slice_dims=(1,),
+        start_index_map=(1,),
+        operand_batching_dims=(0,),
+        start_indices_batching_dims=(0,),
+    )
+
     def look(entry, index):
-        return jnp.take_along_axis(entry, index, axis=1, mode="promise_in_bounds")
-
-    for j in range(SIDE):
+        return lax.gather(
+            entry,
+            index[:, :, None],
+            along_lanes,
+            slice_sizes=(1, 1),
+            mode=lax.GatherScatterMode.PROMISE_IN_BOUNDS,
+        )
+
+    cells = [(z, half) for half in range(rows // 8) for z in range(planes)]
+
+    def look_up_tile(t, slot):
+        at = pl.multiple_of(t * LANES, LANES)
+        for n, (z, half) in enumerate(cells):
+            band = pl.ds(8 * half, 8)
+            sample = field[z + 1, band, pl.ds(at + LANES, LANES)]
+            position = jnp.clip((sample + 3.0) * ((knots - 1) / 6.0), 0.0, knots - 1.0)
+            knot = position.astype(jnp.int32)
+            part = position - knot.astype(jnp.float32)
+            index = (mats[z, band, pl.ds(at, LANES)] * knots + knot) & (LANES - 1)
+            for c, (base, step) in enumerate(tables):
+                looked[slot, n, c] = look(base, index) + part * look(step, index)
+
+    def weigh_tile(t, slot):
+        at = pl.multiple_of(t * LANES, LANES)
+        occupied = flags[0, 0, t].astype(jnp.float32)
+        passed = None
+        for n, (z, half) in enumerate(cells):
+            band = pl.ds(8 * half, 8)
+            kept = jnp.exp(-(looked[slot, n, 3] * occupied))
+            weight = 1.0 - kept if z == 0 else passed * (1.0 - kept)
+            for c in range(3):
+                shade[c, z, band, pl.ds(at, LANES)] = looked[slot, n, c] * weight
+            passed = kept if z == 0 else passed * kept
+            if z == planes - 1:
+                through[band, pl.ds(at, LANES)] = passed
+
+    def look_up(i):
+        for u in range(LOOK_UNROLL):
+            look_up_tile(i * LOOK_UNROLL + u, u)
+
+    def weigh(i):
+        for u in range(LOOK_UNROLL):
+            weigh_tile(i * LOOK_UNROLL + u, u)
+
+    def loaded(j):
         for copy in load(j):
             copy.wait()
 
-        @pl.loop(j * per_chunk, (j + 1) * per_chunk)
-        def _(t):
-            at = pl.multiple_of(t * LANES, LANES)
-            occupied = flags[0, 0, t].astype(jnp.float32)
-            for half in range(rows // 8):
-                band = pl.ds(8 * half, 8)
-                passed = jnp.ones((8, LANES), jnp.float32)
-                for z in range(planes):
-                    sample = field[z + 1, band, pl.ds(at + LANES, LANES)]
-                    position = jnp.clip((sample + 3.0) * ((knots - 1) / 6.0), 0.0, knots - 1.0)
-                    knot = position.astype(jnp.int32)
-                    part = position - knot.astype(jnp.float32)
-                    index = (mats[z, band, pl.ds(at, LANES)] * knots + knot) & (LANES - 1)
-                    values = [look(b, index) + part * look(g, index) for b, g in tables]
-                    kept = jnp.exp(-(values[3] * occupied))
-                    weight = passed * (1.0 - kept)
-                    for c in range(3):
-                        shade[c, z, band, pl.ds(at, LANES)] = values[c] * weight
-                    passed = passed * kept
-                through[band, pl.ds(at, LANES)] = passed
+    steps = per_chunk // LOOK_UNROLL
+
+    def weigh_and_look_up(i):
+        weigh(i - 1)
+        look_up(i)
+
+    loaded(0)
+    look_up(0)
+    pl.loop(1, steps)(weigh_and_look_up)
+    relayed(0)
+    relay_on(1, along_x)
+
+    @pl.loop(1, SIDE)
+    def _(j):
+        loaded(j)
+        pl.loop(j * steps, (j + 1) * steps)(weigh_and_look_up)
+
+    relayed(1)
+    relay_on(2, along_x)
+    weigh(SIDE * steps - 1)
 
     pl.when(has_above)(lambda: row_copy(0).wait_recv())
     pl.when(has_below)(lambda: row_copy(1).wait_recv())
@@ -229,8 +308,7 @@
         return sums
 
     def pack(j):
-        @pl.loop(0, per_chunk)
-        def _(y):
+        def pack_tile(y):
             sums = light_tile(owner(j) * per_chunk + y)
             for c in range(4):
                 first, second = sums[0][c], sums[1][c]
@@ -241,7 +319,14 @@
                     lane < HALF, pltpu.roll(first, HALF, 1), second
                 )
 
+        @pl.loop(0, per_chunk // LIGHT_UNROLL)
+        def _(i):
+            for u in range(LIGHT_UNROLL):
+                pack_tile(i * LIGHT_UNROLL + u)
+
     def join(j):
+        if j == 0:
+            relayed(2)
         core_copy(j).wait_recv()
 
         @pl.loop(0, per_chunk)
@@ -302,6 +387,7 @@
 def on_device(density, materials, occupancy_flags, tf_color, tf_opacity):
     planes, rows, columns = density.shape
     tiles = columns // LANES
+    color = jnp.transpose(tf_color, (1, 0, 2))
     block = (4, 8, LANES)
     f32 = jnp.float32
     dma = pltpu.SemaphoreType.DMA
@@ -310,11 +396,8 @@
         out_shape=jax.ShapeDtypeStruct((4, rows, columns // lax.axis_size("depth")), f32),
         in_specs=[
             pl.BlockSpec(memory_space=pltpu.HBM),
-            pl.BlockSpec(memory_space=pltpu.HBM),
-            pl.BlockSpec(memory_space=pltpu.SMEM),
-            pl.BlockSpec(memory_space=pltpu.VMEM),
-            pl.BlockSpec(memory_space=pltpu.VMEM),
-        ],
+        ]
+        * 5,
         out_specs=pl.BlockSpec(memory_space=pltpu.VMEM),
         scratch_shapes=[
             pltpu.VMEM((planes + 2, rows, columns + 2 * LANES), f32),
@@ -326,6 +409,12 @@
             pltpu.VMEM((3, tiles) + block, f32),
             pltpu.VMEM((CHIPS,) + block, f32),
             pltpu.VMEM((CHIPS,) + block, f32),
+            pltpu.VMEM((LOOK_UNROLL, 2 * planes, 4, 8, LANES), f32),
+            pltpu.SMEM(occupancy_flags.shape, jnp.int32),
+            pltpu.VMEM(color.shape, f32),
+            pltpu.VMEM(tf_opacity.shape, f32),
+            dma((3,)),
+            pltpu.SemaphoreType.REGULAR((3,)),
             dma((2, SIDE)),
             dma((2, SIDE)),
             dma((2, SIDE)),
@@ -340,7 +429,7 @@
             collective_id=0, has_side_effects=True, vmem_limit_bytes=60 << 20
         ),
         name="render",
-    )(density, materials, occupancy_flags, tf_color, tf_opacity)
+    )(density, materials, occupancy_flags, color, tf_opacity)
 
 
 def solution(mesh):

time: 27.1 us -> 23.2 us (0.86)
  Pallas kernels: 24.1 us -> 21.7 us
  local copies, waits for them, and re-layouts: 2.67 us -> 1.38 us
    pallas_call x1, Pallas kernels: 24.1 us -> 21.7 us  [on_device(): pl.pallas_call(kernel, out_shape=jax.ShapeDtypeStruct((4, rows, columns /...]
    unnamed x2 -> x1, local copies, waits for them, and re-layouts: 2.67 us -> 1.38 us
where the time goes in v2:
time: 23.2 us; the launch traced here: 23 us
  Pallas kernels  21.7 us (94%)
  local copies, waits for them, and re-layouts  1.38 us (6%)
    pallas_call x1, Pallas kernels, on_device(): pl.pallas_call(kernel, out_shape=jax.ShapeDtypeStruct((4, rows, columns /...  21.7 us
    unnamed x1, local copies, waits for them, and re-layouts  1.38 us

profile of v2, /device:TPU:1, one launch (start us, length us, event | category | flops | bytes accessed | tf_op | source)
XLA Modules:
  0.0 23.0 jit_solution(15684069028172488452)
XLA Ops:
  0.0 21.7 %render.1 = f32[4,16,64]{2,1,0:T(8,128)} custom-call(f32[4,16,2048]{2,1,0:T(8,128)} %density.1, s32[4,16,2048]{2,1,0:T(8,128)} %materials.1, s32[1,1,16]{2,1,0:T(1,128)} %flags_in.1, f32[3,4,16]{2,1,0:T(4,128)} %bitcast.1, f32[4,16]{1,0:T(4,128)} %opacity_in.1), custom_call_target="tpu_custom_call" | custom-call | tf_op jit(solution)/shard_map/render/pallas_call | solution.py:394
  21.7 1.4 %copy.7 = f32[4,16,64]{2,1,0:T(8,128)} copy(f32[4,16,64]{2,1,0:T(8,128)} %render.1) | data formatting | bytes 32768

commit v3 on v2

--- a/solution.py
+++ b/solution.py
@@ -43,6 +43,7 @@
         return 2 * (lax.rem(x, SIDE) * SIDE + lax.rem(y, SIDE)) + core
 
     along_x = [on_chip(chip_x + step, chip_y) for step in (1, SIDE - 1)]
+    across_x = along_x + [on_chip(chip_x + 2, chip_y)]
     along_y = [on_chip(chip_x, chip_y + step) for step in (1, SIDE - 1)]
     barrier = pltpu.get_barrier_semaphore()
 
@@ -138,10 +139,10 @@
         for other in others:
             tell(relay.at[step], depth=other)
 
-    def relayed(step):
-        pl.semaphore_wait(relay.at[step], 2)
-
-    relay_on(0, along_y)
+    def relayed(step, count):
+        pl.semaphore_wait(relay.at[step], count)
+
+    relay_on(0, along_y + along_x)
 
     @pl.when(jnp.logical_not(has_before))
     def _():
@@ -240,16 +241,14 @@
     loaded(0)
     look_up(0)
     pl.loop(1, steps)(weigh_and_look_up)
-    relayed(0)
-    relay_on(1, along_x)
+    relayed(0, len(along_y + along_x))
+    relay_on(1, across_x)
 
     @pl.loop(1, SIDE)
     def _(j):
         loaded(j)
         pl.loop(j * steps, (j + 1) * steps)(weigh_and_look_up)
 
-    relayed(1)
-    relay_on(2, along_x)
     weigh(SIDE * steps - 1)
 
     pl.when(has_above)(lambda: row_copy(0).wait_recv())
@@ -324,25 +323,22 @@
             for u in range(LIGHT_UNROLL):
                 pack_tile(i * LIGHT_UNROLL + u)
 
+    def over(near, far):
+        return [near[c] + near[3] * far[c] for c in range(3)] + [near[3] * far[3]]
+
     def join(j):
         if j == 0:
-            relayed(2)
+            relayed(1, len(across_x))
         core_copy(j).wait_recv()
-
-        @pl.loop(0, per_chunk)
-        def _(y):
+        for y in range(per_chunk):
             k = owner(j) * SIDE + y
-            near = packed.at[2 * core, j * per_chunk + y]
-            far = packed.at[2 - core, j * per_chunk + y]
-            passed = near[3]
-            for c in range(3):
-                outgoing[k, c] = near[c] + passed * far[c]
-            outgoing[k, 3] = passed * far[3]
-
-        @pl.loop(0, per_chunk)
-        def _(y):
+            near = [packed[2 * core, j * per_chunk + y, c] for c in range(4)]
+            far = [packed[2 - core, j * per_chunk + y, c] for c in range(4)]
+            for c, value in enumerate(over(near, far)):
+                outgoing[k, c] = value
+        for y in range(per_chunk):
             k = owner(j) * SIDE + y
-            pl.when(k != chip)(lambda: piece_copy(k, chip).start())
+            pl.when(k != chip)(lambda k=k: piece_copy(k, chip).start())
 
     for j in range(SIDE):
         pl.when(has_before)(lambda: plane_copy(0, owner(j)).wait_recv())
@@ -359,14 +355,10 @@
     def _(k):
         pl.when(k != chip)(lambda: piece_copy(k, k).wait_recv())
 
-    def over(k, held):
-        passed = held[3]
-        return tuple(held[c] + passed * pieces[k, c] for c in range(3)) + (
-            passed * pieces[k, 3],
-        )
-
-    start = tuple(pieces[0, c] for c in range(4))
-    held = lax.fori_loop(1, CHIPS, over, start)
+    held = [[pieces[k, c] for c in range(4)] for k in range(CHIPS)]
+    while len(held) > 1:
+        held = [over(near, far) for near, far in zip(held[0::2], held[1::2])]
+    held = held[0]
     for c in range(4):
         value = held[c] if c < 3 else 1.0 - held[c]
         image[c, pl.ds(0, 8), :] = value[:, :HALF]
@@ -393,7 +385,7 @@
     dma = pltpu.SemaphoreType.DMA
     return pl.pallas_call(
         kernel,
-        out_shape=jax.ShapeDtypeStruct((4, rows, columns // lax.axis_size("depth")), f32),
+        out_shape=pltpu.VMEM((4, rows, columns // lax.axis_size("depth")), f32),
         in_specs=[
             pl.BlockSpec(memory_space=pltpu.HBM),
         ]
@@ -414,7 +406,7 @@
             pltpu.VMEM(color.shape, f32),
             pltpu.VMEM(tf_opacity.shape, f32),
             dma((3,)),
-            pltpu.SemaphoreType.REGULAR((3,)),
+            pltpu.SemaphoreType.REGULAR((2,)),
             dma((2, SIDE)),
             dma((2, SIDE)),
             dma((2, SIDE)),

time: 23.2 us -> 20.7 us (0.89)
  Pallas kernels: 21.7 us -> 19.9 us
  local copies, waits for them, and re-layouts: 1.38 us -> 0.62 us
    pallas_call x1, Pallas kernels: 21.7 us -> 19.9 us  [on_device(): pl.pallas_call(kernel, out_shape=pltpu.VMEM((4, rows, columns // lax.axis...]
    unnamed x1, local copies, waits for them, and re-layouts: 1.38 us -> 0.62 us
where the time goes in v3:
time: 20.7 us; the launch traced here: 20.5 us
  Pallas kernels  19.9 us (96%)
  local copies, waits for them, and re-layouts  0.62 us (3%)
    pallas_call x1, Pallas kernels, on_device(): pl.pallas_call(kernel, out_shape=pltpu.VMEM((4, rows, columns // lax.axis...  19.9 us
    unnamed x1, local copies, waits for them, and re-layouts  0.62 us

profile of v3, /device:TPU:1, one launch (start us, length us, event | category | flops | bytes accessed | tf_op | source)
XLA Modules:
  0.0 20.5 jit_solution(17436942598329845648)
XLA Ops:
  0.0 19.9 %render.1 = f32[4,16,64]{2,1,0:T(8,128)S(1)} custom-call(f32[4,16,2048]{2,1,0:T(8,128)} %density.1, s32[4,16,2048]{2,1,0:T(8,128)} %materials.1, s32[1,1,16]{2,1,0:T(1,128)} %flags_in.1, f32[3,4,16]{2,1,0:T(4,128)} %bitcast.1, f32[4,16]{1,0:T(4,128)} %opacity_in.1), custom_call_target="tpu_custom_call" | custom-call | tf_op jit(solution)/shard_map/render/pallas_call | solution.py:386
  19.9 0.6 %copy.7 = f32[4,16,64]{2,1,0:T(8,128)} copy(f32[4,16,64]{2,1,0:T(8,128)S(1)} %render.1) | data formatting | bytes 32768

commit v4 on v3

--- a/solution.py
+++ b/solution.py
@@ -12,7 +12,7 @@
 CHIPS = SIDE * SIDE
 LOOK_UNROLL = 4
 LIGHT_UNROLL = 2
-ORDER = (2, 1, 3, 0)
+ORDER = (2, 0, 1, 3)
 
 
 def kernel(
@@ -96,6 +96,10 @@
     )
     pl.semaphore_wait(barrier, expected)
 
+    def wanted(way, j):
+        there = (d + 1 if way == 0 else d - 1) // 2 // SIDE
+        return lax.rem(there + ORDER[j], SIDE)
+
     def plane_copy(way, j):
         j = pl.multiple_of(j * chunk, LANES)
         source = planes - 1 if way == 0 else 0
@@ -132,8 +136,8 @@
     pl.when(has_below)(lambda: row_copy(0).start())
     pl.when(has_above)(lambda: row_copy(1).start())
     for j in range(SIDE):
-        pl.when(has_next)(lambda: plane_copy(0, owner(j)).start())
-        pl.when(has_before)(lambda: plane_copy(1, owner(j)).start())
+        pl.when(has_next)(lambda: plane_copy(0, wanted(0, j)).start())
+        pl.when(has_before)(lambda: plane_copy(1, wanted(1, j)).start())
 
     def relay_on(step, others):
         for other in others:
@@ -351,6 +355,17 @@
 
     pieces[chip] = outgoing[chip]
 
+    pl.when(has_below)(lambda: row_copy(0).wait_send())
+    pl.when(has_above)(lambda: row_copy(1).wait_send())
+    for j in range(SIDE):
+        pl.when(has_next)(lambda: plane_copy(0, wanted(0, j)).wait_send())
+        pl.when(has_before)(lambda: plane_copy(1, wanted(1, j)).wait_send())
+        core_copy(j).wait_send()
+
+    @pl.loop(0, CHIPS)
+    def _(k):
+        pl.when(k != chip)(lambda: piece_copy(k, chip).wait_send())
+
     @pl.loop(0, CHIPS)
     def _(k):
         pl.when(k != chip)(lambda: piece_copy(k, k).wait_recv())
@@ -363,17 +378,6 @@
         value = held[c] if c < 3 else 1.0 - held[c]
         image[c, pl.ds(0, 8), :] = value[:, :HALF]
         image[c, pl.ds(8, 8), :] = pltpu.roll(value, HALF, 1)[:, :HALF]
-
-    pl.when(has_below)(lambda: row_copy(0).wait_send())
-    pl.when(has_above)(lambda: row_copy(1).wait_send())
-    for j in range(SIDE):
-        pl.when(has_next)(lambda: plane_copy(0, owner(j)).wait_send())
-        pl.when(has_before)(lambda: plane_copy(1, owner(j)).wait_send())
-        core_copy(j).wait_send()
-
-    @pl.loop(0, CHIPS)
-    def _(k):
-        pl.when(k != chip)(lambda: piece_copy(k, chip).wait_send())
 
 
 def on_device(density, materials, occupancy_flags, tf_color, tf_opacity):

time: 20.7 us -> 20 us (0.966)
  Pallas kernels: 19.9 us -> 19.2 us
    pallas_call x1, Pallas kernels: 19.9 us -> 19.2 us  [on_device(): pl.pallas_call(kernel, out_shape=pltpu.VMEM((4, rows, columns // lax.axis...]
where the time goes in v4:
time: 20 us; the launch traced here: 19.9 us
  Pallas kernels  19.2 us (96%)
  local copies, waits for them, and re-layouts  0.62 us (3%)
    pallas_call x1, Pallas kernels, on_device(): pl.pallas_call(kernel, out_shape=pltpu.VMEM((4, rows, columns // lax.axis...  19.2 us
    unnamed x1, local copies, waits for them, and re-layouts  0.62 us

profile of v4, /device:TPU:1, one launch (start us, length us, event | category | flops | bytes accessed | tf_op | source)
XLA Modules:
  0.0 19.9 jit_solution(10791290157127785197)
XLA Ops:
  0.0 19.2 %render.1 = f32[4,16,64]{2,1,0:T(8,128)S(1)} custom-call(f32[4,16,2048]{2,1,0:T(8,128)} %density.1, s32[4,16,2048]{2,1,0:T(8,128)} %materials.1, s32[1,1,16]{2,1,0:T(1,128)} %flags_in.1, f32[3,4,16]{2,1,0:T(4,128)} %bitcast.1, f32[4,16]{1,0:T(4,128)} %opacity_in.1), custom_call_target="tpu_custom_call" | custom-call | tf_op jit(solution)/shard_map/render/pallas_call | solution.py:390
  19.3 0.6 %copy.7 = f32[4,16,64]{2,1,0:T(8,128)} copy(f32[4,16,64]{2,1,0:T(8,128)S(1)} %render.1) | data formatting | bytes 32768

commit v5 on v4

--- a/solution.py
+++ b/solution.py
@@ -12,7 +12,6 @@
 CHIPS = SIDE * SIDE
 LOOK_UNROLL = 4
 LIGHT_UNROLL = 2
-ORDER = (2, 0, 1, 3)
 
 
 def kernel(
@@ -96,20 +95,14 @@
     )
     pl.semaphore_wait(barrier, expected)
 
-    def wanted(way, j):
-        there = (d + 1 if way == 0 else d - 1) // 2 // SIDE
-        return lax.rem(there + ORDER[j], SIDE)
-
     def plane_copy(way, j):
-        j = pl.multiple_of(j * chunk, LANES)
         source = planes - 1 if way == 0 else 0
         target = 0 if way == 0 else planes + 1
-        at = j // chunk
         return pltpu.make_async_remote_copy(
-            src_ref=density.at[source, :, pl.ds(j, chunk)],
-            dst_ref=field.at[target, :, pl.ds(j + LANES, chunk)],
-            send_sem=plane_send.at[way, at],
-            recv_sem=plane_recv.at[way, at],
+            src_ref=density.at[source, :, pl.ds(j * chunk, chunk)],
+            dst_ref=field.at[target, :, pl.ds(j * chunk + LANES, chunk)],
+            send_sem=plane_send.at[way, j],
+            recv_sem=plane_recv.at[way, j],
             device_id={"depth": d + 1 if way == 0 else d - 1},
             device_id_type=MESH,
         )
@@ -130,14 +123,11 @@
     has_below = s < strip_count - 1
     has_above = s > 0
 
-    def owner(j):
-        return lax.rem(chip_x + ORDER[j], SIDE)
-
     pl.when(has_below)(lambda: row_copy(0).start())
     pl.when(has_above)(lambda: row_copy(1).start())
     for j in range(SIDE):
-        pl.when(has_next)(lambda: plane_copy(0, wanted(0, j)).start())
-        pl.when(has_before)(lambda: plane_copy(1, wanted(1, j)).start())
+        pl.when(has_next)(lambda: plane_copy(0, j).start())
+        pl.when(has_before)(lambda: plane_copy(1, j).start())
 
     def relay_on(step, others):
         for other in others:
@@ -312,7 +302,7 @@
 
     def pack(j):
         def pack_tile(y):
-            sums = light_tile(owner(j) * per_chunk + y)
+            sums = light_tile(j * per_chunk + y)
             for c in range(4):
                 first, second = sums[0][c], sums[1][c]
                 packed[0, j * per_chunk + y, c] = jnp.where(
@@ -335,18 +325,18 @@
             relayed(1, len(across_x))
         core_copy(j).wait_recv()
         for y in range(per_chunk):
-            k = owner(j) * SIDE + y
+            k = j * per_chunk + y
             near = [packed[2 * core, j * per_chunk + y, c] for c in range(4)]
             far = [packed[2 - core, j * per_chunk + y, c] for c in range(4)]
             for c, value in enumerate(over(near, far)):
                 outgoing[k, c] = value
         for y in range(per_chunk):
-            k = owner(j) * SIDE + y
+            k = j * per_chunk + y
             pl.when(k != chip)(lambda k=k: piece_copy(k, chip).start())
 
     for j in range(SIDE):
-        pl.when(has_before)(lambda: plane_copy(0, owner(j)).wait_recv())
-        pl.when(has_next)(lambda: plane_copy(1, owner(j)).wait_recv())
+        pl.when(has_before)(lambda: plane_copy(0, j).wait_recv())
+        pl.when(has_next)(lambda: plane_copy(1, j).wait_recv())
         pack(j)
         core_copy(j).start()
         if j > 0:
@@ -358,8 +348,8 @@
     pl.when(has_below)(lambda: row_copy(0).wait_send())
     pl.when(has_above)(lambda: row_copy(1).wait_send())
     for j in range(SIDE):
-        pl.when(has_next)(lambda: plane_copy(0, wanted(0, j)).wait_send())
-        pl.when(has_before)(lambda: plane_copy(1, wanted(1, j)).wait_send())
+        pl.when(has_next)(lambda: plane_copy(0, j).wait_send())
+        pl.when(has_before)(lambda: plane_copy(1, j).wait_send())
         core_copy(j).wait_send()
 
     @pl.loop(0, CHIPS)

time: 20 us -> 19.3 us (0.965)
  Pallas kernels: 19.2 us -> 18.5 us
    pallas_call x1, Pallas kernels: 19.2 us -> 18.5 us  [on_device(): pl.pallas_call(kernel, out_shape=pltpu.VMEM((4, rows, columns // lax.axis...]
where the time goes in v5:
time: 19.3 us; the launch traced here: 19.2 us
  Pallas kernels  18.5 us (96%)
  local copies, waits for them, and re-layouts  0.62 us (3%)
    pallas_call x1, Pallas kernels, on_device(): pl.pallas_call(kernel, out_shape=pltpu.VMEM((4, rows, columns // lax.axis...  18.5 us
    unnamed x1, local copies, waits for them, and re-layouts  0.62 us

profile of v5, /device:TPU:1, one launch (start us, length us, event | category | flops | bytes accessed | tf_op | source)
XLA Modules:
  0.0 19.2 jit_solution(2944585014663251189)
XLA Ops:
  0.0 18.5 %render.1 = f32[4,16,64]{2,1,0:T(8,128)S(1)} custom-call(f32[4,16,2048]{2,1,0:T(8,128)} %density.1, s32[4,16,2048]{2,1,0:T(8,128)} %materials.1, s32[1,1,16]{2,1,0:T(1,128)} %flags_in.1, f32[3,4,16]{2,1,0:T(4,128)} %bitcast.1, f32[4,16]{1,0:T(4,128)} %opacity_in.1), custom_call_target="tpu_custom_call" | custom-call | tf_op jit(solution)/shard_map/render/pallas_call | solution.py:380
  18.5 0.6 %copy.7 = f32[4,16,64]{2,1,0:T(8,128)} copy(f32[4,16,64]{2,1,0:T(8,128)S(1)} %render.1) | data formatting | bytes 32768

commit v6 on v5

--- a/solution.py
+++ b/solution.py
@@ -123,11 +123,11 @@
     has_below = s < strip_count - 1
     has_above = s > 0
 
-    pl.when(has_below)(lambda: row_copy(0).start())
-    pl.when(has_above)(lambda: row_copy(1).start())
     for j in range(SIDE):
         pl.when(has_next)(lambda: plane_copy(0, j).start())
         pl.when(has_before)(lambda: plane_copy(1, j).start())
+    pl.when(has_below)(lambda: row_copy(0).start())
+    pl.when(has_above)(lambda: row_copy(1).start())
 
     def relay_on(step, others):
         for other in others:

time: 19.3 us -> 19.3 us (level)
  no operation moved by 1% of the time
where the time goes in v6:
time: 19.3 us; the launch traced here: 19.1 us
  Pallas kernels  18.5 us (96%)
  local copies, waits for them, and re-layouts  0.62 us (3%)
    pallas_call x1, Pallas kernels, on_device(): pl.pallas_call(kernel, out_shape=pltpu.VMEM((4, rows, columns // lax.axis...  18.5 us
    unnamed x1, local copies, waits for them, and re-layouts  0.62 us

profile of v6, /device:TPU:1, one launch (start us, length us, event | category | flops | bytes accessed | tf_op | source)
XLA Modules:
  0.0 19.1 jit_solution(16257188438531775588)
XLA Ops:
  0.0 18.5 %render.1 = f32[4,16,64]{2,1,0:T(8,128)S(1)} custom-call(f32[4,16,2048]{2,1,0:T(8,128)} %density.1, s32[4,16,2048]{2,1,0:T(8,128)} %materials.1, s32[1,1,16]{2,1,0:T(1,128)} %flags_in.1, f32[3,4,16]{2,1,0:T(4,128)} %bitcast.1, f32[4,16]{1,0:T(4,128)} %opacity_in.1), custom_call_target="tpu_custom_call" | custom-call | tf_op jit(solution)/shard_map/render/pallas_call | solution.py:380
  18.5 0.6 %copy.7 = f32[4,16,64]{2,1,0:T(8,128)} copy(f32[4,16,64]{2,1,0:T(8,128)S(1)} %render.1) | data formatting | bytes 32768

commit v7 on v6

--- a/solution.py
+++ b/solution.py
@@ -49,12 +49,12 @@
     def tell(sem, **where):
         pl.semaphore_signal(sem, inc=1, device_id=where, device_id_type=MESH)
 
+    for other in along_x + along_y:
+        tell(barrier, depth=other)
     pl.when(cross_ok)(lambda: tell(barrier, depth=cross))
     pl.when(s > 0)(lambda: tell(barrier, strip=s - 1))
     pl.when(s < strip_count - 1)(lambda: tell(barrier, strip=s + 1))
     tell(barrier, depth=partner)
-    for other in along_x + along_y:
-        tell(barrier, depth=other)
 
     def load(j):
         start = pl.multiple_of(j * chunk, LANES)

time: 19.3 us -> 19.3 us (level)
  no operation moved by 1% of the time
where the time goes in v7:
time: 19.3 us; the launch traced here: 19.1 us
  Pallas kernels  18.5 us (96%)
  local copies, waits for them, and re-layouts  0.62 us (3%)
    pallas_call x1, Pallas kernels, on_device(): pl.pallas_call(kernel, out_shape=pltpu.VMEM((4, rows, columns // lax.axis...  18.5 us
    unnamed x1, local copies, waits for them, and re-layouts  0.62 us

profile of v7, /device:TPU:1, one launch (start us, length us, event | category | flops | bytes accessed | tf_op | source)
XLA Modules:
  0.0 19.1 jit_solution(5159667773897212755)
XLA Ops:
  0.0 18.5 %render.1 = f32[4,16,64]{2,1,0:T(8,128)S(1)} custom-call(f32[4,16,2048]{2,1,0:T(8,128)} %density.1, s32[4,16,2048]{2,1,0:T(8,128)} %materials.1, s32[1,1,16]{2,1,0:T(1,128)} %flags_in.1, f32[3,4,16]{2,1,0:T(4,128)} %bitcast.1, f32[4,16]{1,0:T(4,128)} %opacity_in.1), custom_call_target="tpu_custom_call" | custom-call | tf_op jit(solution)/shard_map/render/pallas_call | solution.py:380
  18.5 0.6 %copy.7 = f32[4,16,64]{2,1,0:T(8,128)} copy(f32[4,16,64]{2,1,0:T(8,128)S(1)} %render.1) | data formatting | bytes 32768
